TPU v7x, 512 devices: a whole 4x4x16 slice. The times are simulated.
512 devices in a mesh: batch: 32 (over z, core), row: 4 (over y), col: 4 (over x).
Axes of the slice: x: 4, y: 4, z: 16, core: 2. Of those that a mesh axis runs over, the one named last changes fastest.
Arguments:
- image_tokens: bfloat16 [128, 256, 3072], P('batch', ('row', 'col')), may hold values from -36 to 36
- text_tokens: bfloat16 [128, 128, 3072], P('batch', ('row', 'col')), may hold values from -36 to 36
- modulation: float32 [128, 7, 3072], P('batch'), may hold values from -3.5 to 3.5
- qkv_weight: bfloat16 [3072, 12, 384], P('col', 'row'), may hold values from -0.109375 to 0.109375
- kv_weight: bfloat16 [3072, 12, 256], P('col', 'row'), may hold values from -0.109375 to 0.109375
- norm_gains: float32 [3, 128], replicated, may hold values from 1 to 2.2
- out_weight: bfloat16 [12, 128, 3072], P('row', None, 'col'), may hold values from -0.15625 to 0.15625
- final_weight: bfloat16 [3072, 64], replicated, may hold values from -0.109375 to 0.109375
- text_lengths: int32 [128], P('batch'), may hold values from 1 to 128, as said below
- partner: int32 [128], P('batch'), may hold values from 0 to 127, as said below
- guidance: float32 [128], P('batch'), may hold values from 1.5 to 4.5
- step_size: float32 [128], P('batch'), may hold values from -0.3 to -0.05
- latent: float32 [128, 256, 64], P('batch', ('row', 'col')), may hold values from -6 to 6
Outputs:
- next_latent: float32 [128, 256, 64], P('batch', ('row', 'col'))
Inputs may be any that keep to these rules, and one draw needn't show every extreme that they name: `text_lengths`: some sequence has all 128 text tokens live. partner[partner[s]] = s and partner[s] != s for every sequence s.
All inputs are finite; a program needn't handle non-finite values.
Results may differ from a plain program's by a relative error of at most 0.007.
Values may be sent and summed in bfloat16 or wider, within the bound.
No kernel may reach another device: no remote copies, remote signals or barrier semaphores. Data moves between devices by JAX's collectives and lax.ppermute only.
A program may use at most 64 MiB of HBM per device.

v0:
```python
import math
import jax
import jax.numpy as jnp
from jax import lax
from jax.sharding import PartitionSpec as P

epsilon = 1e-06


def layer_norm(values):
    center = jnp.mean(values, axis=-1, keepdims=True)
    spread = jnp.mean((values - center) * (values - center), axis=-1, keepdims=True)
    return (values - center) * lax.rsqrt(spread + epsilon)


def modulate(values, shift, scale):
    return layer_norm(values) * (1.0 + scale[:, None, :]) + shift[:, None, :]


def head_norm(values, gain):
    return values * lax.rsqrt(jnp.mean(values * values, axis=-1, keepdims=True) + epsilon) * gain


def attend(queries, all_keys, all_values, live, head_size):
    scores = jnp.einsum(
        "sqhe,skhe->shqk", queries, all_keys, preferred_element_type=jnp.float32
    ) / math.sqrt(head_size)
    expo = jnp.exp(scores) * live[:, None, None, :]
    totals = jnp.sum(expo, axis=-1)
    mixed = jnp.einsum(
        "shqk,skhe->sqhe", expo.astype(jnp.bfloat16), all_values, preferred_element_type=jnp.float32
    )
    return (mixed / jnp.transpose(totals, (0, 2, 1))[..., None]).astype(jnp.bfloat16)


def per_device(
    image_tokens,
    text_tokens,
    modulation,
    qkv_weight,
    kv_weight,
    norm_gains,
    out_weight,
    final_weight,
    text_lengths,
    partner,
    guidance,
    step_size,
    latent,
):
    count = image_tokens.shape[0]
    head_size = norm_gains.shape[1]
    block_width = qkv_weight.shape[0]
    image_mod = modulate(
        image_tokens.astype(jnp.float32), modulation[:, 0], modulation[:, 1]
    ).astype(jnp.bfloat16)
    text_mod = modulate(text_tokens.astype(jnp.float32), modulation[:, 3], modulation[:, 4]).astype(
        jnp.bfloat16
    )
    image_whole, text_whole = (
        lax.all_gather(image_mod, ("row", "col"), axis=1, tiled=True),
        lax.all_gather(text_mod, ("row", "col"), axis=1, tiled=True),
    )
    offset = lax.axis_index("col") * block_width
    image_all = lax.dynamic_slice_in_dim(image_whole, offset, block_width, 2)
    text_all = lax.dynamic_slice_in_dim(text_whole, offset, block_width, 2)
    qkv_term = jnp.einsum(
        "std,dhe->sthe", image_all, qkv_weight, preferred_element_type=jnp.float32
    )
    kv_term = jnp.einsum("std,dhe->sthe", text_all, kv_weight, preferred_element_type=jnp.float32)
    qkv_sum, kv_sum = (
        lax.psum(qkv_term.astype(jnp.bfloat16), "col").astype(jnp.float32),
        lax.psum(kv_term.astype(jnp.bfloat16), "col").astype(jnp.float32),
    )
    queries = head_norm(qkv_sum[..., :head_size], norm_gains[0]).astype(jnp.bfloat16)
    image_keys = head_norm(qkv_sum[..., head_size : 2 * head_size], norm_gains[1]).astype(
        jnp.bfloat16
    )
    image_values = qkv_sum[..., 2 * head_size :].astype(jnp.bfloat16)
    text_keys = head_norm(kv_sum[..., :head_size], norm_gains[2]).astype(jnp.bfloat16)
    text_values = kv_sum[..., head_size:].astype(jnp.bfloat16)
    text_count = text_keys.shape[1]
    image_count = image_keys.shape[1]
    all_keys = jnp.concatenate([text_keys, image_keys], axis=1)
    all_values = jnp.concatenate([text_values, image_values], axis=1)
    text_live = (jnp.arange(text_count, dtype=jnp.int32)[None, :] < text_lengths[:, None]).astype(
        jnp.float32
    )
    live = jnp.concatenate([text_live, jnp.ones((count, image_count), jnp.float32)], axis=1)
    heads = attend(queries, all_keys, all_values, live, head_size)
    out_term = jnp.einsum("sqhe,hed->sqd", heads, out_weight, preferred_element_type=jnp.float32)
    attn_rows = lax.psum_scatter(
        out_term.astype(jnp.bfloat16), "row", scatter_dimension=1, tiled=True
    )
    attn_tokens = lax.all_to_all(attn_rows, "col", split_axis=1, concat_axis=2, tiled=True)
    residual = image_tokens.astype(jnp.float32) + modulation[:, 2][:, None, :] * attn_tokens.astype(
        jnp.float32
    )
    final_in = modulate(residual, modulation[:, 5], modulation[:, 6]).astype(jnp.bfloat16)
    velocity = jnp.einsum("std,dc->stc", final_in, final_weight, preferred_element_type=jnp.float32)
    token_rows = velocity.shape[1]
    channels = velocity.shape[2]
    flat_velocity = velocity.reshape(count, token_rows * channels)
    every_velocity, every_guidance = (
        lax.all_gather(flat_velocity, "batch", axis=0, tiled=True),
        lax.all_gather(guidance, "batch", axis=0, tiled=True),
    )
    mate = jnp.take(every_velocity, partner, axis=0).reshape(velocity.shape)
    own_index = lax.axis_index("batch") * count + jnp.arange(count, dtype=jnp.int32)
    is_cond = own_index < partner
    cond_vel = jnp.where(is_cond[:, None, None], velocity, mate)
    uncond_vel = jnp.where(is_cond[:, None, None], mate, velocity)
    scale_guide = jnp.where(is_cond, guidance, jnp.take(every_guidance, partner))
    guided = uncond_vel + scale_guide[:, None, None] * (cond_vel - uncond_vel)
    ratio = jnp.sqrt(
        (jnp.mean(cond_vel * cond_vel, axis=-1, keepdims=True) + epsilon)
        / (jnp.mean(guided * guided, axis=-1, keepdims=True) + epsilon)
    )
    return latent + step_size[:, None, None] * guided * (0.7 * ratio + 0.3)


def solution(mesh):
    return jax.shard_map(
        per_device,
        mesh=mesh,
        in_specs=(
            P("batch", ("row", "col"), None),
            P("batch", ("row", "col"), None),
            P("batch", None, None),
            P("col", "row", None),
            P("col", "row", None),
            P(),
            P("row", None, "col"),
            P(),
            P("batch"),
            P("batch"),
            P("batch"),
            P("batch"),
            P("batch", ("row", "col"), None),
        ),
        out_specs=P("batch", ("row", "col"), None),
        check_vma=False,
    )
```

profile of v0, /device:TPU:1, one launch (start us, length us, event | category | flops | bytes accessed | tf_op | source)
XLA Modules:
  0.0 376.6 jit_solution(10970847019949007939)
XLA Ops:
  6.5 1.2 convert_reduce_fusion.1
  7.7 1.1 fusion.42
  8.9 1.0 slice_bitcast_fusion.3
  9.9 1.8 fusion.45
  11.6 0.0 all-gather.4.cloned.1.call-update
  11.7 0.0 all-gather.6.cloned.1.call-start
  11.7 1.1 convert_reduce_fusion
  12.8 0.2 fusion.27
  13.1 1.0 fusion.30
  14.1 0.0 all-reduce.5.cloned.1.call-start
  14.2 65.4 %all-gather.4.cloned.1.call-done = bf16[4,128,3072]{2,1,0:T(8,128)(2,1)} async-done(((bf16[4,8,3072]{2,1,0:T(8,128)(2,1)}), bf16[4,128,3072]{2,1,0:T(8,128)(2,1)}) %all-gather.4.cloned.1.call-update) | async-done | bytes 3145744 | tf_op jit(solution)/shard_map/all_gather | solution.py:62
  79.6 3.2 convolution_convert_fusion.1
  82.7 75.8 %all-gather.6.cloned.1.call-done = bf16[4,256,3072]{2,1,0:T(8,128)(2,1)} async-done(((bf16[4,16,3072]{2,1,0:T(8,128)(2,1)}), bf16[4,256,3072]{2,1,0:T(8,128)(2,1)}) %all-gather.6.cloned.1.call-update) | async-done | bytes 6291472 | tf_op jit(solution)/shard_map/all_gather | solution.py:61
  158.5 5.0 %convolution_convert_fusion = bf16[4,256,3,384]{3,1,2,0:T(8,128)(2,1)} fusion(bf16[768,3,384]{2,0,1:T(8,128)(2,1)S(1)} %copy-done, bf16[4,256,3072]{2,1,0:T(8,128)(2,1)} %all-gather.6.cloned.1.call-done, s32[]{:T(128)S(6)} %select_n.32), kind=kOutput, calls=%fused_computation.9 | convolution fusion | flops 1813118976 | bytes 5701636 | tf_op jit(solution)/shard_map/std,dhe->sthe/dot_general | solution.py:67
  163.6 0.0 reduce-scatter.2.cloned.1.call-start
  163.6 0.6 copy-done.9
  164.2 0.1 iota_compare_fusion
  164.3 90.3 %all-reduce.5.cloned.1.call-done = (bf16[4,256,3,384]{3,1,2,0:T(8,128)(2,1)}, bf16[4,128,3,256]{3,1,2,0:T(8,128)(2,1)}) async-done(((bf16[4,256,3,384]{3,1,2,0:T(8,128)(2,1)}, bf16[4,128,3,256]{3,1,2,0:T(8,128)(2,1)}), (bf16[4,256,3,384]{3,1,2,0:T(8,128)(2,1)}, bf16[4,128,3,256]{3,1,2,0:T(8,128)(2,1)})) %all-reduce.5.cloned.1.call-update) | async-done | bytes 3145744 | tf_op jit(solution)/shard_map/psum | solution.py:72
  254.6 1.4 fusion.31
  256.0 1.0 slice.70
  257.1 1.2 slice.71
  258.3 0.4 convert_element_type.65
  258.7 0.9 multiply_reduce_fusion.1
  259.6 0.2 copy-done.3
  259.9 0.3 fusion.33
  260.2 0.5 multiply_convert_fusion
  260.6 2.8 fusion
  263.4 5.8 %bitcast_convert_fusion = bf16[4,256,768]{2,1,0:T(8,128)(2,1)} fusion(f32[4,3,256,384]{3,2,1,0:T(8,128)} %get-tuple-element.25, f32[4,384]{1,0:T(4,128)S(1)} %pad_convert_fusion, bf16[4,256,3,128]{3,1,2,0:T(8,128)(2,1)S(1)} %slice.71, bf16[4,128,3,128]{3,1,2,0:T(8,128)(2,1)S(1)} %slice.70, f32[4,256,3]{1,2,0:T(4,128)S(1)} %bitcast.60, ...), kind=kOutput, calls=%fused_computation.5 | convolution fusion | flops 913440768 | bytes 8079360 | tf_op jit(solution)/shard_map/sqhe,hed->sqd/dot_general | solution.py:91
  269.2 1.3 dynamic-slice
  271.2 0.2 dynamic-update-slice
  271.4 48.1 %all-reduce.1 = f32[128]{0:T(128)S(1)} all-reduce(f32[128]{0:T(128)S(1)} %dynamic-update-slice), channel_id=1, replica_groups=mesh['batch'=32,'row'=4,'col'=4] {'batch'}, use_global_device_ids=true, to_apply=%add.1 | all-reduce | flops 128 | bytes 1024
  319.6 0.0 reduce-scatter.2.cloned.1.call-done
  319.6 2.0 copy.18
  321.6 3.5 all-to-all-start
  325.1 0.6 gather_fusion.1
  325.8 5.5 %all-to-all-done = bf16[4,64,768]{2,0,1:T(4,128)(2,1)S(1)} async-done(((bf16[4,64,768]{2,0,1:T(4,128)(2,1)}), bf16[4,64,768]{2,0,1:T(4,128)(2,1)S(1)}, u32[]{:S(2)}, u32[]{:S(2)}) %all-to-all-start) | async-done | bytes 393248 | tf_op jit(solution)/shard_map/all_to_all | solution.py:95
  331.3 1.2 copy.26
  332.5 1.5 reshape.109
  334.0 0.2 fusion.52
  334.2 0.3 multiply_reduce_fusion.2
  334.5 1.4 fusion.46
  335.9 0.1 reshape.132
  336.0 32.3 %all-gather = f32[32,4,1024]{2,1,0:T(4,128)S(1)} all-gather(f32[1,4,1024]{2,1,0:T(4,128)S(1)} %reshape.132), channel_id=1, replica_groups=mesh['batch'=32,'row'=4,'col'=4] {'batch'}, dimensions={0}, use_global_device_ids=true | all-gather | bytes 540672 | tf_op jit(solution)/shard_map/all_gather | solution.py:105
  368.3 0.2 reshape.133
  368.5 0.6 gather_fusion
  369.1 0.1 gather.11
  369.2 0.2 multiply_reduce_fusion.3
  369.4 0.7 multiply_add_fusion
  (38 shorter events, 0.2 us)
Async XLA Ops:
  6.5 152.0 %copy-start = (bf16[768,3,384]{2,0,1:T(8,128)(2,1)S(1)}, bf16[768,3,384]{2,0,1:T(8,128)(2,1)}, u32[]{:S(2)}) copy-start(bf16[768,3,384]{2,0,1:T(8,128)(2,1)} %param.16) | copy-start | bytes 5308420
  6.5 6.3 %copy-start.1 = (bf16[4,16,3072]{2,1,0:T(8,128)(2,1)S(1)}, bf16[4,16,3072]{2,1,0:T(8,128)(2,1)}, u32[]{:S(2)}) copy-start(bf16[4,16,3072]{2,1,0:T(8,128)(2,1)} %param.13) | copy-start | bytes 1179652
  6.5 73.0 %all-gather.4.cloned.1.call-start = ((), (), s32[]{:S(2)}) async-start(), calls=%async_computation.2 | async-start | bytes 3342336 | tf_op jit(solution)/shard_map/all_gather | solution.py:62
  11.7 146.9 %all-gather.6.cloned.1.call-start = ((), (), s32[]{:S(2)}) async-start(), calls=%async_computation.3 | async-start | bytes 6684672 | tf_op jit(solution)/shard_map/all_gather | solution.py:61
  14.1 240.5 %all-reduce.5.cloned.1.call-start = ((), (), s32[]{:S(2)}) async-start(), calls=%async_computation.5 | async-start | bytes 6291456 | tf_op jit(solution)/shard_map/psum | solution.py:72
  163.5 0.7 copy-start.9
  163.5 0.7 copy-start.5
  163.6 156.0 %reduce-scatter.2.cloned.1.call-start = ((), (), s32[]{:S(2)}) async-start(), calls=%async_computation.4 | async-start | bytes 1966080 | tf_op jit(solution)/shard_map/reduce_scatter | solution.py:92
  254.6 3.7 copy-start.2
  258.7 1.1 copy-start.3
  263.4 7.7 %copy-start.7 = (f32[4]{0:T(128)S(1)}, f32[4]{0:T(128)}, u32[]{:S(2)}) copy-start(f32[4]{0:T(128)} %param.23) | copy-start | bytes 52
  263.4 56.1 %copy-start.8 = (s32[4]{0:T(128)S(1)}, s32[4]{0:T(128)}, u32[]{:S(2)}) copy-start(s32[4]{0:T(128)} %param.22) | copy-start | bytes 52
  321.6 9.7 %all-to-all-start = ((bf16[4,64,768]{2,0,1:T(4,128)(2,1)}), bf16[4,64,768]{2,0,1:T(4,128)(2,1)S(1)}, u32[]{:S(2)}, u32[]{:S(2)}) async-start(bf16[4,64,768]{2,0,1:T(4,128)(2,1)} %copy.18), calls=%async_computation.1 | async-start | bytes 786432 | tf_op jit(solution)/shard_map/all_to_all | solution.py:95
  334.2 35.1 %copy-start.4 = (f32[4,16,64]{2,1,0:T(8,128)S(1)}, f32[4,16,64]{2,1,0:T(8,128)}, u32[]{:S(2)}) copy-start(f32[4,16,64]{2,1,0:T(8,128)} %param.25) | copy-start | bytes 49156
  334.2 35.1 %copy-start.6 = (f32[4]{0:T(128)S(1)}, f32[4]{0:T(128)}, u32[]{:S(2)}) copy-start(f32[4]{0:T(128)} %param.24) | copy-start | bytes 52
Sparse Core Ops, SparseCore 0:
  11.8 67.7 all-gather.3
  82.6 75.8 all-gather.5
  163.7 90.8 all-reduce.4
  269.3 32.5 reduce-scatter.1
where the time goes:
time: 377 us
  waiting for transfers between devices  237 us (63%)
  blocking collectives  80.4 us (21%)
  matrix products  18.2 us (5%)
  between operations  14 us (4%)
  other arithmetic  12.5 us (3%)
  local copies, waits for them, and re-layouts  10.9 us (3%)
    psum x1, waiting for transfers between devices, per_device(): lax.psum(qkv_term.astype(jnp.bfloat16), 'col').astype(jnp.float32)  90.3 us
    all_gather x1, waiting for transfers between devices, per_device(): lax.all_gather(image_mod, ('row', 'col'), axis=1, tiled=True)  75.8 us
    all_gather x1, waiting for transfers between devices, per_device(): lax.all_gather(text_mod, ('row', 'col'), axis=1, tiled=True)  65.4 us
    unnamed x1, blocking collectives  48.1 us
    all_gather x1, blocking collectives, per_device(): lax.all_gather(flat_velocity, 'batch', axis=0, tiled=True)  32.3 us
  transfers between devices with their start and end apart: 5, of which 4 were waited for; matrix products, arithmetic and copies ran while one was open for 2% of the time, Pallas kernels for 0%

commit v1 on v0

--- a/solution.py
+++ b/solution.py
@@ -69,7 +69,7 @@
     )
     kv_term = jnp.einsum("std,dhe->sthe", text_all, kv_weight, preferred_element_type=jnp.float32)
     qkv_sum, kv_sum = (
-        lax.psum(qkv_term.astype(jnp.bfloat16), "col").astype(jnp.float32),
+        jnp.sum(lax.all_gather(qkv_term.astype(jnp.bfloat16), "col"), axis=0).astype(jnp.float32),
         lax.psum(kv_term.astype(jnp.bfloat16), "col").astype(jnp.float32),
     )
     queries = head_norm(qkv_sum[..., :head_size], norm_gains[0]).astype(jnp.bfloat16)

time: 377 us -> 451 us (1.20)
  waiting for transfers between devices: 237 us -> 302 us
  other arithmetic: 12.5 us -> 23 us
    all_gather x0 -> x1, waiting for transfers between devices: none -> 101 us  [per_device(): lax.all_gather(qkv_term.astype(jnp.bfloat16), 'col')]
    psum x1, waiting for transfers between devices: 90.3 us -> 54.4 us  [per_device(): lax.psum(kv_term.astype(jnp.bfloat16), 'col').astype(jnp.float32)]
    reduce_sum x0 -> x1, other arithmetic: none -> 7.34 us  [per_device(): jnp.sum(lax.all_gather(qkv_term.astype(jnp.bfloat16), 'col'), axis=0)]
  transfers between devices with their start and end apart: 5 -> 6, of which waited for: 4 -> 5; matrix products, arithmetic and copies ran while one was open for 2% -> 4% of each run, Pallas kernels for 0% -> 0%
where the time goes in v1:
time: 451 us; the launch traced here: 450 us
  waiting for transfers between devices  302 us (67%)
  blocking collectives  80.4 us (18%)
  other arithmetic  23 us (5%)
  matrix products  18.1 us (4%)
  between operations  14 us (3%)
  local copies, waits for them, and re-layouts  8.47 us (2%)
    all_gather x1, waiting for transfers between devices, per_device(): lax.all_gather(qkv_term.astype(jnp.bfloat16), 'col')  101 us
    all_gather x1, waiting for transfers between devices, per_device(): lax.all_gather(image_mod, ('row', 'col'), axis=1, tiled=True)  75.7 us
    all_gather x1, waiting for transfers between devices, per_device(): lax.all_gather(text_mod, ('row', 'col'), axis=1, tiled=True)  65.4 us
    psum x1, waiting for transfers between devices, per_device(): lax.psum(kv_term.astype(jnp.bfloat16), 'col').astype(jnp.float32)  54.4 us
    unnamed x1, blocking collectives  48 us
    all_gather x1, blocking collectives, per_device(): lax.all_gather(flat_velocity, 'batch', axis=0, tiled=True)  32.4 us
  transfers between devices with their start and end apart: 6, of which 5 were waited for; matrix products, arithmetic and copies ran while one was open for 4% of the time, Pallas kernels for 0%

profile of v1, /device:TPU:1, one launch (start us, length us, event | category | flops | bytes accessed | tf_op | source)
XLA Modules:
  0.0 450.0 jit_solution(8894481704465383309)
XLA Ops:
  6.5 1.2 convert_reduce_fusion.1
  7.7 1.1 fusion.42
  8.9 1.0 slice_bitcast_fusion.3
  9.9 1.7 fusion.45
  11.6 0.0 all-gather.8.cloned.1.call-start
  11.7 1.1 convert_reduce_fusion
  12.8 0.2 fusion.27
  13.1 1.0 fusion.30
  14.1 0.0 all-gather.8.cloned.1.call-update
  14.1 0.0 all-reduce.4.cloned.1.call-start
  14.1 65.4 %all-gather.6.cloned.1.call-done = bf16[4,128,3072]{2,1,0:T(8,128)(2,1)} async-done(((bf16[4,8,3072]{2,1,0:T(8,128)(2,1)}), bf16[4,128,3072]{2,1,0:T(8,128)(2,1)}) %all-gather.6.cloned.1.call-update) | async-done | bytes 3145744 | tf_op jit(solution)/shard_map/all_gather | solution.py:62
  79.5 3.2 convolution_convert_fusion.1
  82.8 0.0 all-gather.10.cloned.1.call-start
  82.8 75.7 %all-gather.8.cloned.1.call-done = bf16[4,256,3072]{2,1,0:T(8,128)(2,1)} async-done(((bf16[4,16,3072]{2,1,0:T(8,128)(2,1)}), bf16[4,256,3072]{2,1,0:T(8,128)(2,1)}) %all-gather.8.cloned.1.call-update) | async-done | bytes 6291472 | tf_op jit(solution)/shard_map/all_gather | solution.py:61
  158.5 5.0 %convolution_convert_fusion = bf16[4,256,3,384]{3,1,2,0:T(8,128)(2,1)} fusion(bf16[768,3,384]{2,0,1:T(8,128)(2,1)S(1)} %copy-done, bf16[4,256,3072]{2,1,0:T(8,128)(2,1)} %all-gather.8.cloned.1.call-done, s32[]{:T(128)S(6)} %select_n.32), kind=kOutput, calls=%fused_computation.9 | convolution fusion | flops 1813118976 | bytes 5701636 | tf_op jit(solution)/shard_map/std,dhe->sthe/dot_general | solution.py:67
  163.5 0.0 reduce-scatter.2.cloned.1.call-start
  163.6 0.6 copy-done.8
  164.2 0.1 iota_compare_fusion
  164.3 54.4 %all-reduce.4.cloned.1.call-done = bf16[4,128,3,256]{3,1,2,0:T(8,128)(2,1)} async-done(((bf16[4,128,3,256]{3,1,2,0:T(8,128)(2,1)}), bf16[4,128,3,256]{3,1,2,0:T(8,128)(2,1)}) %all-reduce.4.cloned.1.call-update) | async-done | bytes 786448 | tf_op jit(solution)/shard_map/psum | solution.py:73
  218.7 1.3 fusion.31
  220.0 2.0 fusion.33
  222.0 101.0 %all-gather.10.cloned.1.call-done = bf16[16,256,3,384]{3,1,2,0:T(8,128)(2,1)} async-done(((bf16[4,256,3,384]{3,1,2,0:T(8,128)(2,1)}), bf16[16,256,3,384]{3,1,2,0:T(8,128)(2,1)}) %all-gather.10.cloned.1.call-update) | async-done | bytes 9437200 | tf_op jit(solution)/shard_map/all_gather | solution.py:72
  322.9 7.3 %reduce_sum.124 = bf16[4,256,3,384]{3,1,2,0:T(8,128)(2,1)} reduce(bf16[4,4,256,3,384]{4,2,3,1,0:T(8,128)(2,1)} %bitcast.59, bf16[]{:T(256)} %constant.77.clone.1), dimensions={0}, to_apply=%region_5.0 | reduce | flops 3538944 | bytes 11796482 | tf_op jit(solution)/shard_map/reduce_sum | solution.py:72
  330.3 2.1 convert_element_type.67
  332.4 0.9 multiply_reduce_fusion.1
  333.4 0.5 multiply_convert_fusion
  333.9 2.8 fusion
  336.7 5.7 %bitcast_convert_fusion = bf16[4,256,768]{2,1,0:T(8,128)(2,1)} fusion(f32[4,3,256,384]{3,2,1,0:T(8,128)} %get-tuple-element.23, f32[4,384]{1,0:T(4,128)S(1)} %pad_convert_fusion, bf16[4,256,3,128]{3,1,2,0:T(8,128)(2,1)S(1)} %slice-done, bf16[4,128,3,128]{3,1,2,0:T(8,128)(2,1)S(1)} %slice-done.1, f32[4,256,3]{1,2,0:T(4,128)S(1)} %bitcast.62, ...), kind=kOutput, calls=%fused_computation.5 | convolution fusion | flops 913440768 | bytes 8079360 | tf_op jit(solution)/shard_map/sqhe,hed->sqd/dot_general | solution.py:91
  342.5 1.3 dynamic-slice
  344.4 0.2 dynamic-update-slice
  344.7 48.0 %all-reduce.1 = f32[128]{0:T(128)S(1)} all-reduce(f32[128]{0:T(128)S(1)} %dynamic-update-slice), channel_id=1, replica_groups=mesh['batch'=32,'row'=4,'col'=4] {'batch'}, use_global_device_ids=true, to_apply=%add.1 | all-reduce | flops 128 | bytes 1024
  392.7 0.0 reduce-scatter.2.cloned.1.call-done
  392.7 2.0 copy.18
  394.7 3.7 all-to-all-start
  398.4 0.6 gather_fusion.1
  399.1 5.6 %all-to-all-done = bf16[4,64,768]{2,0,1:T(4,128)(2,1)S(1)} async-done(((bf16[4,64,768]{2,0,1:T(4,128)(2,1)}), bf16[4,64,768]{2,0,1:T(4,128)(2,1)S(1)}, u32[]{:S(2)}, u32[]{:S(2)}) %all-to-all-start) | async-done | bytes 393248 | tf_op jit(solution)/shard_map/all_to_all | solution.py:95
  404.6 1.2 copy.26
  405.8 1.5 reshape.109
  407.4 0.2 fusion.52
  407.6 0.2 multiply_reduce_fusion.2
  407.8 1.4 fusion.46
  409.2 0.1 reshape.133
  409.3 32.4 %all-gather.1 = f32[32,4,1024]{2,1,0:T(4,128)S(1)} all-gather(f32[1,4,1024]{2,1,0:T(4,128)S(1)} %reshape.133), channel_id=1, replica_groups=mesh['batch'=32,'row'=4,'col'=4] {'batch'}, dimensions={0}, use_global_device_ids=true | all-gather | bytes 540672 | tf_op jit(solution)/shard_map/all_gather | solution.py:105
  441.7 0.2 reshape.134
  441.9 0.6 gather_fusion
  442.5 0.1 gather.11
  442.6 0.2 multiply_reduce_fusion.3
  442.8 0.7 multiply_add_fusion
  (43 shorter events, 0.3 us)
Async XLA Ops:
  6.5 152.0 %copy-start = (bf16[768,3,384]{2,0,1:T(8,128)(2,1)S(1)}, bf16[768,3,384]{2,0,1:T(8,128)(2,1)}, u32[]{:S(2)}) copy-start(bf16[768,3,384]{2,0,1:T(8,128)(2,1)} %param.16) | copy-start | bytes 5308420
  6.5 6.3 %copy-start.1 = (bf16[4,16,3072]{2,1,0:T(8,128)(2,1)S(1)}, bf16[4,16,3072]{2,1,0:T(8,128)(2,1)}, u32[]{:S(2)}) copy-start(bf16[4,16,3072]{2,1,0:T(8,128)(2,1)} %param.13) | copy-start | bytes 1179652
  6.5 73.0 %all-gather.6.cloned.1.call-start = ((), (), s32[]{:S(2)}) async-start(), calls=%async_computation.2 | async-start | bytes 3342336 | tf_op jit(solution)/shard_map/all_gather | solution.py:62
  11.6 146.9 %all-gather.8.cloned.1.call-start = ((), (), s32[]{:S(2)}) async-start(), calls=%async_computation.4 | async-start | bytes 6684672 | tf_op jit(solution)/shard_map/all_gather | solution.py:61
  14.1 204.6 %all-reduce.4.cloned.1.call-start = ((), (), s32[]{:S(2)}) async-start(), calls=%async_computation.3 | async-start | bytes 1572864 | tf_op jit(solution)/shard_map/psum | solution.py:73
  82.8 240.2 %all-gather.10.cloned.1.call-start = ((), (), s32[]{:S(2)}) async-start(), calls=%async_computation.6 | async-start | bytes 11796480 | tf_op jit(solution)/shard_map/all_gather | solution.py:72
  163.5 0.7 copy-start.8
  163.5 0.7 copy-start.4
  163.5 229.1 %reduce-scatter.2.cloned.1.call-start = ((), (), s32[]{:S(2)}) async-start(), calls=%async_computation.5 | async-start | bytes 1966080 | tf_op jit(solution)/shard_map/reduce_scatter | solution.py:92
  332.4 1.4 copy-start.2
  333.9 2.8 slice-start
  333.9 2.8 slice-start.1
  336.7 7.7 %copy-start.6 = (f32[4]{0:T(128)S(1)}, f32[4]{0:T(128)}, u32[]{:S(2)}) copy-start(f32[4]{0:T(128)} %param.23) | copy-start | bytes 52
  336.7 55.9 %copy-start.7 = (s32[4]{0:T(128)S(1)}, s32[4]{0:T(128)}, u32[]{:S(2)}) copy-start(s32[4]{0:T(128)} %param.22) | copy-start | bytes 52
  394.7 9.9 %all-to-all-start = ((bf16[4,64,768]{2,0,1:T(4,128)(2,1)}), bf16[4,64,768]{2,0,1:T(4,128)(2,1)S(1)}, u32[]{:S(2)}, u32[]{:S(2)}) async-start(bf16[4,64,768]{2,0,1:T(4,128)(2,1)} %copy.18), calls=%async_computation.1 | async-start | bytes 786432 | tf_op jit(solution)/shard_map/all_to_all | solution.py:95
  407.6 35.2 %copy-start.3 = (f32[4,16,64]{2,1,0:T(8,128)S(1)}, f32[4,16,64]{2,1,0:T(8,128)}, u32[]{:S(2)}) copy-start(f32[4,16,64]{2,1,0:T(8,128)} %param.25) | copy-start | bytes 49156
  407.6 35.2 %copy-start.5 = (f32[4]{0:T(128)S(1)}, f32[4]{0:T(128)}, u32[]{:S(2)}) copy-start(f32[4]{0:T(128)} %param.24) | copy-start | bytes 52
Sparse Core Ops, SparseCore 0:
  11.8 67.7 all-gather.5
  82.6 75.8 all-gather.7
  160.9 57.7 all-reduce.3
  220.6 102.2 all-gather.9
  342.6 33.7 reduce-scatter.1
